TPU v7x, 256 devices: a whole 4x4x8 slice. The times are simulated.
256 devices in a mesh: seq: 32 (over y, x, core), tensor: 8 (over z).
Axes of the slice: x: 4, y: 4, z: 8, core: 2. Of those that a mesh axis runs over, the one named last changes fastest.
Arguments:
- hidden: bfloat16 [8192, 3072], P('seq'), may hold values from -6 to 6
- attention_norm_gain: bfloat16 [3072], replicated, may hold values from 0.099609375 to 1.8984375
- query_key_value_weight: bfloat16 [3, 3072, 3072], P(None, None, 'tensor'), may hold values from -0.109375 to 0.109375
- output_weight: bfloat16 [3072, 3072], P('tensor'), may hold values from -0.3125 to 0.3125
- adapter_down_weight: bfloat16 [3072, 16], P('tensor'), may hold values from -0.3125 to 0.3125
- adapter_up_weight: bfloat16 [16, 3072], replicated, may hold values from -1.5 to 1.5
- final_norm_gain: bfloat16 [3072], replicated, may hold values from 0.099609375 to 1.8984375
- head: bfloat16 [16384, 3072], P('tensor', 'seq')
- prompt_key_slots: bfloat16 [64, 128, 3072], P('seq', None, 'tensor')
- prompt_value_slots: bfloat16 [64, 128, 3072], P('seq', None, 'tensor'), may hold values from -6 to 6
- counts: int32 [8], replicated, may hold values from 1 to 8, as said below
- page_slot_index: int32 [64], replicated, may hold values from 0 to 63, each once
- owner: int32 [128], replicated, may hold values from 0 to 7, as said below
- targets: int32 [8192], P('seq'), may hold values from 0 to 16383
Outputs:
- logprob_policy: float32 [8192], P('seq')
- logprob_reference: float32 [8192], P('seq')
Inputs may be any that keep to these rules, and one draw needn't show every extreme that they name: `counts`: every prompt fills 1 to 8 pages, and some prompt fills exactly 8. `page_slot_index`: slot s is held by index s // 2 of seq; every slot is named once. `owner`: every prompt owns exactly 16 rollouts, placed anywhere.
All inputs are finite; a program needn't handle non-finite values.
Results may differ from a plain program's by a relative error of at most 0.014.
The roundings to bfloat16 on the way count: a program that leaves them out, or rounds other values in their place, can miss the bound.
Values may be sent and summed in bfloat16 or wider, within the bound.
No kernel may reach another device: no remote copies, remote signals or barrier semaphores. Data moves between devices by JAX's collectives and lax.ppermute only.
A program may use at most 192 MiB of HBM per device.

v0:
```python
import math
import jax
import jax.numpy as jnp
from jax import lax
from jax.sharding import PartitionSpec as P

HEAD_WIDTH = 96
LEN = 64
PAGE = 128
MAXP = 8
EPSILON = 1e-05
NEGATIVE = -1e30


def rms_norm(values, gain):
    mean_sq = jnp.mean(values * values, axis=-1, keepdims=True)
    return (values * lax.rsqrt(mean_sq + EPSILON) * gain.astype(jnp.float32)).astype(jnp.bfloat16)


def rotate(values, positions):
    half_width = values.shape[-1] // 2
    frequency = 10000.0 ** (-jnp.arange(half_width, dtype=jnp.float32) * 2.0 / values.shape[-1])
    angles = positions.astype(jnp.float32)[:, None] * frequency[None, :]
    cosine = jnp.cos(angles)[:, None, :]
    sinus = jnp.sin(angles)[:, None, :]
    first = values[..., :half_width]
    second = values[..., half_width:]
    return jnp.concatenate(
        [first * cosine - second * sinus, second * cosine + first * sinus], axis=-1
    )


def local(
    hidden,
    attention_norm_gain,
    query_key_value_weight,
    output_weight,
    adapter_down_weight,
    adapter_up_weight,
    final_norm_gain,
    head,
    prompt_key_slots,
    prompt_value_slots,
    counts,
    page_slot_index,
    owner,
    targets,
):
    tok_rows = hidden.shape[0]
    rollouts_here = tok_rows // LEN
    heads_here = output_weight.shape[0] // HEAD_WIDTH
    width_here = heads_here * HEAD_WIDTH
    score_scale = 1.0 / math.sqrt(HEAD_WIDTH)
    stream = hidden.astype(jnp.float32)
    normed = rms_norm(stream, attention_norm_gain)
    groups_iota = jnp.arange(counts.shape[0], dtype=jnp.int32)
    my_groups = lax.dynamic_slice_in_dim(
        owner, lax.axis_index("seq") * rollouts_here, rollouts_here, 0
    )
    tok_group = jnp.repeat(my_groups, LEN)
    group_pages = jnp.sum(
        jnp.where(tok_group[:, None] == groups_iota[None, :], counts[None, :], 0), axis=1
    )
    positions = group_pages * PAGE + jnp.arange(tok_rows, dtype=jnp.int32) % LEN
    queries = rotate(
        jnp.dot(normed, query_key_value_weight[0], preferred_element_type=jnp.float32).reshape(
            tok_rows, heads_here, HEAD_WIDTH
        ),
        positions,
    ).astype(jnp.bfloat16)
    keys_new = rotate(
        jnp.dot(normed, query_key_value_weight[1], preferred_element_type=jnp.float32).reshape(
            tok_rows, heads_here, HEAD_WIDTH
        ),
        positions,
    ).astype(jnp.bfloat16)
    values_new = (
        jnp.dot(normed, query_key_value_weight[2], preferred_element_type=jnp.float32)
        .astype(jnp.bfloat16)
        .reshape(tok_rows, heads_here, HEAD_WIDTH)
    )
    query_roll = queries.reshape(rollouts_here, LEN, heads_here, HEAD_WIDTH)
    key_roll = keys_new.reshape(rollouts_here, LEN, heads_here, HEAD_WIDTH)
    value_roll = values_new.reshape(rollouts_here, LEN, heads_here, HEAD_WIDTH)
    causal = jnp.arange(LEN, dtype=jnp.int32)[None, :] <= jnp.arange(LEN, dtype=jnp.int32)[:, None]
    own_scores = (
        jnp.einsum("rthd,rkhd->rhtk", query_roll, key_roll, preferred_element_type=jnp.float32)
        * score_scale
    )
    own_max = jnp.max(jnp.where(causal, own_scores, NEGATIVE), axis=-1)
    own_weights = jnp.where(causal, jnp.exp(own_scores - own_max[..., None]), 0.0)
    own_total = jnp.sum(own_weights, axis=-1)
    own_summed = jnp.einsum(
        "rhtk,rkhd->rhtd",
        own_weights.astype(jnp.bfloat16),
        value_roll,
        preferred_element_type=jnp.float32,
    )
    start_max = jnp.transpose(own_max, (1, 0, 2)).reshape(heads_here, tok_rows)
    start_total = jnp.transpose(own_total, (1, 0, 2)).reshape(heads_here, tok_rows)
    start_summed = jnp.transpose(own_summed, (1, 0, 2, 3)).reshape(heads_here, tok_rows, HEAD_WIDTH)
    entries = jnp.arange(page_slot_index.shape[0], dtype=jnp.int32)
    key_piece = lax.all_gather(prompt_key_slots, "seq", axis=0, tiled=True)
    value_piece = lax.all_gather(prompt_value_slots, "seq", axis=0, tiled=True)
    piece_slots = key_piece.shape[0]
    slot_ids = jnp.arange(piece_slots, dtype=jnp.int32)
    matches = page_slot_index[None, :] == slot_ids[:, None]
    slot_group = jnp.sum(jnp.where(matches, entries // MAXP, 0), axis=1)
    slot_page = jnp.sum(jnp.where(matches, entries % MAXP, 0), axis=1)
    slot_count = jnp.sum(
        jnp.where(slot_group[:, None] == groups_iota[None, :], counts[None, :], 0), axis=1
    )
    key_live = jnp.repeat(slot_page < slot_count, PAGE)
    key_group = jnp.repeat(slot_group, PAGE)
    visible = (tok_group[:, None] == key_group[None, :]) & key_live[None, :]
    totals = start_total
    summed = start_summed
    keys_flat = key_piece.reshape(piece_slots * PAGE, heads_here, HEAD_WIDTH)
    values_flat = value_piece.reshape(piece_slots * PAGE, heads_here, HEAD_WIDTH)
    scores = (
        jnp.einsum("thd,khd->htk", queries, keys_flat, preferred_element_type=jnp.float32)
        * score_scale
    )
    block_max = jnp.max(jnp.where(visible[None], scores, NEGATIVE), axis=-1)
    new_max = jnp.maximum(start_max, block_max)
    weights = jnp.where(visible[None], jnp.exp(scores - new_max[..., None]), 0.0)
    rescale = jnp.exp(start_max - new_max)
    totals = totals * rescale + jnp.sum(weights, axis=-1)
    summed = summed * rescale[..., None] + jnp.einsum(
        "htk,khd->htd",
        weights.astype(jnp.bfloat16),
        values_flat,
        preferred_element_type=jnp.float32,
    )
    attention_output = (summed / totals[..., None]).astype(jnp.bfloat16)
    attention_output = jnp.transpose(attention_output, (1, 0, 2)).reshape(tok_rows, width_here)
    branch_part = jnp.dot(attention_output, output_weight, preferred_element_type=jnp.float32)
    adapter_portion = jnp.dot(
        attention_output, adapter_down_weight, preferred_element_type=jnp.float32
    )
    branch_sum, adapter_delta = (
        lax.psum(branch_part.astype(jnp.bfloat16), "tensor").astype(jnp.float32),
        lax.psum(adapter_portion.astype(jnp.bfloat16), "tensor").astype(jnp.float32),
    )
    reference_hidden = stream + branch_sum
    policy_hidden = reference_hidden + jnp.dot(
        adapter_delta, adapter_up_weight.astype(jnp.float32), precision=lax.Precision.HIGHEST
    )
    normed_ref = rms_norm(reference_hidden, final_norm_gain)
    normed_pol = rms_norm(policy_hidden, final_norm_gain)
    head_rows = lax.all_gather(head, "seq", axis=1, tiled=True)
    stacked = jnp.concatenate([normed_pol, normed_ref], axis=0)
    logits = lax.dot_general(
        stacked, head_rows, (((1,), (1,)), ((), ())), preferred_element_type=jnp.float32
    )
    vocab_here = head_rows.shape[0]
    target_ids = jnp.concatenate([targets, targets], axis=0) - lax.axis_index("tensor") * vocab_here
    is_target = jnp.arange(vocab_here, dtype=jnp.int32)[None, :] == target_ids[:, None]
    picked = jnp.sum(jnp.where(is_target, logits, 0.0), axis=1)
    local_max = jnp.max(logits, axis=1)
    whole_max = lax.pmax(local_max, "tensor")
    local_total = jnp.sum(jnp.exp(logits - whole_max[:, None]), axis=1)
    whole_total, whole_picked = lax.psum((local_total, picked), "tensor")
    log_probs = whole_picked - whole_max - jnp.log(whole_total)
    return (log_probs[:tok_rows], log_probs[tok_rows:])


def solution(mesh):
    return jax.shard_map(
        local,
        mesh=mesh,
        in_specs=(
            P("seq", None),
            P(),
            P(None, None, "tensor"),
            P("tensor", None),
            P("tensor", None),
            P(),
            P(),
            P("tensor", "seq"),
            P("seq", None, "tensor"),
            P("seq", None, "tensor"),
            P(),
            P(),
            P(),
            P("seq"),
        ),
        out_specs=(P("seq"), P("seq")),
        check_vma=False,
    )
```

profile of v0, /device:TPU:2, one launch (start us, length us, event | category | flops | bytes accessed | tf_op | source)
XLA Modules:
  0.0 396.3 jit_solution(10816526754883917571)
XLA Ops:
  7.2 0.0 all-gather.4.cloned.1.call-start
  7.2 0.7 all-gather.4.cloned.1.call-update
  7.9 0.0 all-gather.6.cloned.1.call-start
  8.0 0.7 all-gather.6.cloned.1.call-update
  8.7 0.0 all-reduce.3.cloned.1.call-start
  8.7 0.7 dynamic_slice.3
  9.4 0.1 broadcast_in_dim.114
  9.5 0.1 eq.78
  9.6 0.7 convert_element_type.55
  10.3 5.1 %slice_bitcast_fusion = (bf16[384,3072]{0,1:T(8,128)(2,1)}, bf16[384,3072]{0,1:T(8,128)(2,1)}) fusion(bf16[3,3072,384]{2,1,0:T(8,128)(2,1)} %param.16), kind=kLoop, calls=%fused_computation.29 | loop fusion | bytes 9437184 | tf_op jit(solution)/shard_map/dot_general | solution.py:72
  15.4 4.3 %copy.69 = bf16[384,3072]{1,0:T(8,128)(2,1)} copy(bf16[384,3072]{0,1:T(8,128)(2,1)} %get-tuple-element.10) | data formatting | bytes 4718592 | tf_op jit(solution)/shard_map/dot_general | solution.py:72
  19.7 4.3 %copy.66 = bf16[384,3072]{1,0:T(8,128)(2,1)} copy(bf16[384,3072]{0,1:T(8,128)(2,1)} %get-tuple-element.11) | data formatting | bytes 4718592 | tf_op jit(solution)/shard_map/dot_general | solution.py:66
  24.0 0.1 select_reduce_fusion.5
  24.1 1.8 fusion.5
  25.9 0.3 multiply_cosine_fusion
  26.2 3.2 fusion.15
  29.4 0.1 copy-done.5
  29.6 0.9 fusion.17
  30.5 0.1 subtract_convert_fusion
  30.6 0.1 concatenate.32
  30.7 0.2 copy.67
  31.0 0.1 concatenate.33
  31.1 0.2 copy.68
  31.3 0.1 concatenate.35
  31.5 0.9 copy.70
  32.4 0.1 concatenate.36
  32.5 0.9 copy.71
  33.4 1.5 select_reduce_fusion.2
  34.9 0.1 fusion.31
  35.0 0.1 reshape.237
  35.1 0.1 reshape.234
  35.2 3.2 fusion.22
  38.4 0.2 reshape_reshape.3
  38.6 0.3 convolution_bitcast_fusion
  38.9 0.2 copy.77
  39.1 0.1 select_reduce_fusion.3
  39.2 0.1 select_reduce_fusion.6
  39.3 0.1 broadcast_bitcast_fusion.1
  39.4 0.1 broadcast_bitcast_fusion
  39.5 2.8 compare_and_fusion
  42.3 24.7 %all-gather.4.cloned.1.call-done = bf16[64,128,384]{2,1,0:T(8,128)(2,1)} async-done(((bf16[2,128,384]{2,1,0:T(8,128)(2,1)}), bf16[64,128,384]{2,1,0:T(8,128)(2,1)}) %all-gather.4.cloned.1.call-update) | async-done | bytes 6291472 | tf_op jit(solution)/shard_map/all_gather | solution.py:103
  67.0 9.0 %copy.76 = bf16[64,128,384]{1,0,2:T(8,128)(2,1)} copy(bf16[64,128,384]{2,1,0:T(8,128)(2,1)} %all-gather.4.cloned.1.call-done) | data formatting | bytes 12582912 | tf_op jit(solution)/shard_map/all_gather | solution.py:103
  76.0 10.3 %reshape.235 = bf16[8192,4,96]{0,2,1:T(8,128)(2,1)} reshape(bf16[64,128,384]{1,0,2:T(8,128)(2,1)} %copy.76) | data formatting | bytes 12582912 | tf_op jit(solution)/shard_map/reshape | solution.py:118
  86.3 36.4 %all-gather.6.cloned.1.call-done = bf16[64,128,384]{2,1,0:T(8,128)(2,1)} async-done(((bf16[2,128,384]{2,1,0:T(8,128)(2,1)}), bf16[64,128,384]{2,1,0:T(8,128)(2,1)}) %all-gather.6.cloned.1.call-update) | async-done | bytes 6291472 | tf_op jit(solution)/shard_map/all_gather | solution.py:104
  122.7 9.1 %copy.78 = bf16[64,128,384]{1,0,2:T(8,128)(2,1)} copy(bf16[64,128,384]{2,1,0:T(8,128)(2,1)} %all-gather.6.cloned.1.call-done) | data formatting | bytes 12582912 | tf_op jit(solution)/shard_map/all_gather | solution.py:104
  131.8 10.3 %reshape.236 = bf16[8192,4,96]{0,2,1:T(8,128)(2,1)} reshape(bf16[64,128,384]{1,0,2:T(8,128)(2,1)} %copy.78) | data formatting | bytes 12582912 | tf_op jit(solution)/shard_map/reshape | solution.py:119
  142.1 18.0 %select_reduce_fusion = (f32[4,256]{1,0:T(4,128)S(1)}, f32[4,256,8192]{2,1,0:T(8,128)}) fusion(pred[256,8192]{1,0:T(8,128)(4,1)} %compare_and_fusion, bf16[8192,4,96]{0,2,1:T(8,128)(2,1)} %reshape.235, bf16[256,4,48]{0,2,1:T(8,128)(2,1)S(1)} %get-tuple-element.16, bf16[256,4,48]{0,2,1:T(8,128)(2,1)S(1)} %copy-done.7), kind=kOutput, calls=%fused_computation.1 | convolution fusion | flops 1636170752 | bytes 42143744 | tf_op jit(solution)/shard_map/thd,khd->htk/dot_general | solution.py:121
  160.1 15.2 %fusion = f32[4,256]{1,0:T(4,128)S(1)} fusion(f32[4,256,8192]{2,1,0:T(8,128)} %get-tuple-element.27, f32[4,256]{1,0:T(4,128)S(1)} %max.15, pred[256,8192]{1,0:T(8,128)(4,1)S(1)} %copy-done.4), kind=kLoop, calls=%fused_computation.2 | loop fusion | flops 33553408 | bytes 35659776 | tf_op jit(solution)/shard_map/reduce_sum | solution.py:128
  175.4 15.2 %fusion.28 = bf16[4,256,96]{1,2,0:T(8,128)(2,1)S(1)} fusion(bf16[8192,4,96]{0,2,1:T(8,128)(2,1)} %reshape.236, f32[4,256,8192]{2,1,0:T(8,128)} %get-tuple-element.27, f32[4,256]{1,0:T(4,128)S(1)} %max.15, pred[256,8192]{1,0:T(8,128)(4,1)S(1)} %copy-done.4, f32[4,256,96]{1,2,0:T(8,128)S(1)} %copy.77, f32[4,256]{1,0:T(4,128)S(1)} %get-tuple-element.8, ...), kind=kOutput, calls=%fused_computation.40 | convolution fusion | flops 1644560384 | bytes 42545152 | tf_op jit(solution)/shard_map/htk,khd->htd/dot_general | solution.py:129
  190.7 2.1 convolution_convert_fusion
  192.8 0.0 all-gather.8.cloned.1.call-start
  192.9 0.5 all-gather.8.cloned.1.call-update
  193.5 0.1 convolution_convert_fusion.1
  193.6 17.8 %psum.29 = bf16[256,16]{0,1:T(8,128)(2,1)S(1)} all-reduce(bf16[256,16]{0,1:T(8,128)(2,1)S(1)} %convolution_convert_fusion.1), channel_id=1, replica_groups=mesh['seq'=32,'tensor'=8] {'tensor'}, use_global_device_ids=true, to_apply=%region_10.11 | all-reduce | flops 4096 | bytes 16384 | tf_op jit(solution)/shard_map/psum | solution.py:143
  211.4 60.1 %all-reduce.3.cloned.1.call-done = bf16[256,3072]{1,0:T(8,128)(2,1)} async-done(((bf16[256,3072]{1,0:T(8,128)(2,1)}), bf16[256,3072]{1,0:T(8,128)(2,1)}) %all-reduce.3.cloned.1.call-update) | async-done | bytes 1572880 | tf_op jit(solution)/shard_map/psum | solution.py:142
  271.6 2.9 multiply_reduce_fusion.1
  274.5 0.6 multiply_reduce_fusion
  275.1 3.0 multiply_convert_fusion.1
  278.1 63.1 %all-gather.8.cloned.1.call-done = bf16[2048,3072]{0,1:T(8,128)(2,1)} async-done(((bf16[2048,96]{0,1:T(8,128)(2,1)}), bf16[2048,3072]{0,1:T(8,128)(2,1)}) %all-gather.8.cloned.1.call-update) | async-done | bytes 12582928 | tf_op jit(solution)/shard_map/all_gather | solution.py:151
  341.2 11.9 %fusion.60 = (f32[512]{0:T(512)S(1)}, f32[512,2048]{1,0:T(8,128)}) fusion(bf16[2048,3072]{0,1:T(8,128)(2,1)} %all-gather.8.cloned.1.call-done, bf16[256,3072]{1,0:T(8,128)(2,1)} %get-tuple-element.19, bf16[256,3072]{1,0:T(8,128)(2,1)} %get-tuple-element.18), kind=kOutput, calls=%fused_computation.99 | convolution fusion | flops 6449790464 | bytes 19924992 | tf_op jit(solution)/shard_map/dot_general | solution.py:153
  353.1 17.4 %pmax.7 = f32[512]{0:T(512)S(1)} all-reduce(f32[512]{0:T(512)S(1)} %get-tuple-element.30), channel_id=1, replica_groups=mesh['seq'=32,'tensor'=8] {'tensor'}, use_global_device_ids=true, to_apply=%region_16.17 | all-reduce | flops 512 | bytes 4096 | tf_op jit(solution)/shard_map/pmax | solution.py:161
  370.5 3.6 select_reduce_fusion.1
  374.1 15.0 %all-reduce = (f32[512]{0:T(512)S(1)}, f32[512]{0:T(512)S(1)}) all-reduce(f32[512]{0:T(512)S(1)} %get-tuple-element.3, f32[512]{0:T(512)S(1)} %get-tuple-element.2), channel_id=1, replica_groups=mesh['seq'=32,'tensor'=8] {'tensor'}, use_global_device_ids=true, to_apply=%region_18.19 | all-reduce | flops 1024 | bytes 8192 | tf_op jit(solution)/shard_map/psum | solution.py:163
  389.2 0.6 fusion.59
  (44 shorter events, 0.2 us)
Async XLA Ops:
  7.2 183.5 %copy-start = (bf16[384,3072]{1,0:T(8,128)(2,1)S(1)}, bf16[384,3072]{1,0:T(8,128)(2,1)}, u32[]{:S(2)}) copy-start(bf16[384,3072]{1,0:T(8,128)(2,1)} %param.17) | copy-start | bytes 7077892
  7.2 59.8 %all-gather.4.cloned.1.call-start = ((), (), s32[]{:S(2)}) async-start(), calls=%async_computation | async-start | bytes 6488064 | tf_op jit(solution)/shard_map/all_gather | solution.py:103
  7.9 114.8 %all-gather.6.cloned.1.call-start = ((), (), s32[]{:S(2)}) async-start(), calls=%async_computation.1 | async-start | bytes 6488064 | tf_op jit(solution)/shard_map/all_gather | solution.py:104
  8.7 262.9 %all-reduce.3.cloned.1.call-start = ((), (), s32[]{:S(2)}) async-start(), calls=%async_computation.2 | async-start | bytes 3145728 | tf_op jit(solution)/shard_map/psum | solution.py:142
  19.7 4.3 %copy-start.13 = (s32[8]{0:T(128)S(1)}, s32[8]{0:T(128)}, u32[]{:S(2)}) copy-start(s32[8]{0:T(128)} %param.24) | copy-start | bytes 100
  26.2 3.3 copy-start.1
  26.2 3.4 copy-start.5
  30.6 2.8 copy-start.6
  38.4 0.7 copy-start.12
  131.8 10.3 %copy-start.7 = (bf16[256,4,48]{0,2,1:T(8,128)(2,1)S(1)}, bf16[256,4,48]{0,2,1:T(8,128)(2,1)}, u32[]{:S(2)}) copy-start(bf16[256,4,48]{0,2,1:T(8,128)(2,1)} %copy-done.6) | copy-start | bytes 294916
  142.1 18.0 %copy-start.4 = (pred[256,8192]{1,0:T(8,128)(4,1)S(1)}, pred[256,8192]{1,0:T(8,128)(4,1)}, u32[]{:S(2)}) copy-start(pred[256,8192]{1,0:T(8,128)(4,1)} %compare_and_fusion) | copy-start | bytes 6291460
  190.6 2.8 copy-start.10
  190.6 2.8 copy-start.11
  190.6 2.8 copy-start.9
  190.7 80.9 %copy-start.8 = (bf16[16,3072]{1,0:T(8,128)(2,1)S(1)}, bf16[16,3072]{1,0:T(8,128)(2,1)}, u32[]{:S(2)}) copy-start(bf16[16,3072]{1,0:T(8,128)(2,1)} %param.19) | copy-start | bytes 294916
  192.8 148.3 %all-gather.8.cloned.1.call-start = ((), (), s32[]{:S(2)}) async-start(), calls=%async_computation.3 | async-start | bytes 12976128 | tf_op jit(solution)/shard_map/all_gather | solution.py:151
  271.6 2.9 copy-start.2
  271.6 2.9 copy-start.3
Sparse Core Ops, SparseCore 0:
  10.6 56.3 all-gather.3
  69.5 53.1 all-gather.5
  193.0 78.5 all-reduce.2
  274.0 67.1 all-gather.7
where the time goes:
time: 398 us; the launch traced here: 396 us
  waiting for transfers between devices  186 us (47%)
  matrix products  59.3 us (15%)
  local copies, waits for them, and re-layouts  57.6 us (14%)
  blocking collectives  50.3 us (13%)
  other arithmetic  28.6 us (7%)
  between operations  14.1 us (4%)
    all_gather x1, waiting for transfers between devices, local(): head_rows = lax.all_gather(head, 'seq', axis=1, tiled=True)  63.1 us
    psum x1, waiting for transfers between devices, local(): lax.psum(branch_part.astype(jnp.bfloat16), 'tensor').astype(jnp.float32)  60.1 us
    all_gather x1, waiting for transfers between devices, local(): value_piece = lax.all_gather(prompt_value_slots, 'seq', axis=0, tiled=True)  36.4 us
    all_gather x1, waiting for transfers between devices, local(): key_piece = lax.all_gather(prompt_key_slots, 'seq', axis=0, tiled=True)  24.7 us
    dot_general x1, matrix products, local(): jnp.einsum('thd,khd->htk', queries, keys_flat, preferred_element_type=jnp...  18 us
    psum x1, blocking collectives, local(): lax.psum(adapter_portion.astype(jnp.bfloat16), 'tensor').astype(jnp.float32)  17.8 us
    pmax x1, blocking collectives, local(): whole_max = lax.pmax(local_max, 'tensor')  17.4 us
    reduce_sum x1, other arithmetic, local(): totals = totals * rescale + jnp.sum(weights, axis=-1)  15.2 us
  transfers between devices with their start and end apart: 4, of which 4 were waited for; matrix products, arithmetic and copies ran while one was open for 15% of the time, Pallas kernels for 0%

commit v1 on v0

--- a/solution.py
+++ b/solution.py
@@ -139,7 +139,9 @@
         attention_output, adapter_down_weight, preferred_element_type=jnp.float32
     )
     branch_sum, adapter_delta = (
-        lax.psum(branch_part.astype(jnp.bfloat16), "tensor").astype(jnp.float32),
+        jnp.sum(lax.all_gather(branch_part.astype(jnp.bfloat16), "tensor"), axis=0).astype(
+            jnp.float32
+        ),
         lax.psum(adapter_portion.astype(jnp.bfloat16), "tensor").astype(jnp.float32),
     )
     reference_hidden = stream + branch_sum

time: 398 us -> 452 us (1.14)
  waiting for transfers between devices: 186 us -> 231 us
  other arithmetic: 28.6 us -> 37.5 us
    all_gather x0 -> x1, waiting for transfers between devices: none -> 115 us  [local(): lax.all_gather(branch_part.astype(jnp.bfloat16), 'tensor')]
    psum x1 -> x0, waiting for transfers between devices: 60.1 us -> none  [local(): lax.psum(branch_part.astype(jnp.bfloat16), 'tensor').astype(jnp.float32)]
    all_gather x1, waiting for transfers between devices: 63.1 us -> 53.4 us  [local(): head_rows = lax.all_gather(head, 'seq', axis=1, tiled=True)]
    reduce_sum x0 -> x1, other arithmetic: none -> 8.81 us  [local(): jnp.sum(lax.all_gather(branch_part.astype(jnp.bfloat16), 'tensor'), axis=0)]
where the time goes in v1:
time: 452 us; the launch traced here: 450 us
  waiting for transfers between devices  231 us (51%)
  matrix products  59.4 us (13%)
  local copies, waits for them, and re-layouts  57.6 us (13%)
  blocking collectives  50.7 us (11%)
  other arithmetic  37.5 us (8%)
  between operations  14.1 us (3%)
    all_gather x1, waiting for transfers between devices, local(): lax.all_gather(branch_part.astype(jnp.bfloat16), 'tensor')  115 us
    all_gather x1, waiting for transfers between devices, local(): head_rows = lax.all_gather(head, 'seq', axis=1, tiled=True)  53.4 us
    all_gather x1, waiting for transfers between devices, local(): value_piece = lax.all_gather(prompt_value_slots, 'seq', axis=0, tiled=True)  36.4 us
    all_gather x1, waiting for transfers between devices, local(): key_piece = lax.all_gather(prompt_key_slots, 'seq', axis=0, tiled=True)  24.7 us
    psum x1, blocking collectives, local(): lax.psum(adapter_portion.astype(jnp.bfloat16), 'tensor').astype(jnp.float32)  18.2 us
    dot_general x1, matrix products, local(): jnp.einsum('thd,khd->htk', queries, keys_flat, preferred_element_type=jnp...  18 us
    pmax x1, blocking collectives, local(): whole_max = lax.pmax(local_max, 'tensor')  17.4 us
    reduce_sum x1, other arithmetic, local(): totals = totals * rescale + jnp.sum(weights, axis=-1)  15.2 us
  transfers between devices with their start and end apart: 4, of which 4 were waited for; matrix products, arithmetic and copies ran while one was open for 15% of the time, Pallas kernels for 0%

profile of v1, /device:TPU:2, one launch (start us, length us, event | category | flops | bytes accessed | tf_op | source)
XLA Modules:
  0.0 450.4 jit_solution(6196841426294762335)
XLA Ops:
  7.2 0.7 all-gather.6.cloned.1.call-update
  7.9 0.0 all-gather.8.cloned.1.call-start
  8.0 0.7 all-gather.8.cloned.1.call-update
  8.7 0.0 all-gather.12.cloned.1.call-start
  8.7 0.7 dynamic_slice.3
  9.4 0.1 broadcast_in_dim.114
  9.5 0.1 eq.78
  9.6 0.7 convert_element_type.57
  10.3 5.1 %slice_bitcast_fusion = (bf16[384,3072]{0,1:T(8,128)(2,1)}, bf16[384,3072]{0,1:T(8,128)(2,1)}) fusion(bf16[3,3072,384]{2,1,0:T(8,128)(2,1)} %param.16), kind=kLoop, calls=%fused_computation.29 | loop fusion | bytes 9437184 | tf_op jit(solution)/shard_map/dot_general | solution.py:72
  15.4 4.3 copy.69
  19.7 4.3 copy.66
  24.0 0.1 select_reduce_fusion.5
  24.1 1.8 fusion.5
  25.9 0.3 multiply_cosine_fusion
  26.2 3.2 fusion.15
  29.4 0.1 copy-done.5
  29.6 0.9 fusion.17
  30.5 0.1 subtract_convert_fusion
  30.6 0.1 concatenate.32
  30.7 0.2 copy.67
  31.0 0.1 concatenate.33
  31.1 0.2 copy.68
  31.3 0.1 concatenate.35
  31.5 0.9 copy.70
  32.4 0.1 concatenate.36
  32.5 0.9 copy.71
  33.4 1.5 select_reduce_fusion.2
  34.9 0.1 fusion.31
  35.0 0.1 reshape.237
  35.1 0.1 reshape.234
  35.2 3.2 fusion.22
  38.4 0.2 reshape_reshape.3
  38.6 0.3 convolution_bitcast_fusion
  38.9 0.2 copy.77
  39.1 0.1 select_reduce_fusion.3
  39.2 0.1 select_reduce_fusion.6
  39.3 0.1 broadcast_bitcast_fusion.1
  39.4 0.1 broadcast_bitcast_fusion
  39.5 2.8 compare_and_fusion
  42.3 24.7 %all-gather.6.cloned.1.call-done = bf16[64,128,384]{2,1,0:T(8,128)(2,1)} async-done(((bf16[2,128,384]{2,1,0:T(8,128)(2,1)}), bf16[64,128,384]{2,1,0:T(8,128)(2,1)}) %all-gather.6.cloned.1.call-update) | async-done | bytes 6291472 | tf_op jit(solution)/shard_map/all_gather | solution.py:103
  67.0 9.0 %copy.76 = bf16[64,128,384]{1,0,2:T(8,128)(2,1)} copy(bf16[64,128,384]{2,1,0:T(8,128)(2,1)} %all-gather.6.cloned.1.call-done) | data formatting | bytes 12582912 | tf_op jit(solution)/shard_map/all_gather | solution.py:103
  76.0 10.3 %reshape.235 = bf16[8192,4,96]{0,2,1:T(8,128)(2,1)} reshape(bf16[64,128,384]{1,0,2:T(8,128)(2,1)} %copy.76) | data formatting | bytes 12582912 | tf_op jit(solution)/shard_map/reshape | solution.py:118
  86.3 36.4 %all-gather.8.cloned.1.call-done = bf16[64,128,384]{2,1,0:T(8,128)(2,1)} async-done(((bf16[2,128,384]{2,1,0:T(8,128)(2,1)}), bf16[64,128,384]{2,1,0:T(8,128)(2,1)}) %all-gather.8.cloned.1.call-update) | async-done | bytes 6291472 | tf_op jit(solution)/shard_map/all_gather | solution.py:104
  122.7 9.1 %copy.78 = bf16[64,128,384]{1,0,2:T(8,128)(2,1)} copy(bf16[64,128,384]{2,1,0:T(8,128)(2,1)} %all-gather.8.cloned.1.call-done) | data formatting | bytes 12582912 | tf_op jit(solution)/shard_map/all_gather | solution.py:104
  131.8 10.3 %reshape.236 = bf16[8192,4,96]{0,2,1:T(8,128)(2,1)} reshape(bf16[64,128,384]{1,0,2:T(8,128)(2,1)} %copy.78) | data formatting | bytes 12582912 | tf_op jit(solution)/shard_map/reshape | solution.py:119
  142.1 18.0 %select_reduce_fusion = (f32[4,256]{1,0:T(4,128)S(1)}, f32[4,256,8192]{2,1,0:T(8,128)}) fusion(pred[256,8192]{1,0:T(8,128)(4,1)} %compare_and_fusion, bf16[8192,4,96]{0,2,1:T(8,128)(2,1)} %reshape.235, bf16[256,4,48]{0,2,1:T(8,128)(2,1)S(1)} %get-tuple-element.16, bf16[256,4,48]{0,2,1:T(8,128)(2,1)S(1)} %copy-done.7), kind=kOutput, calls=%fused_computation.1 | convolution fusion | flops 1636170752 | bytes 42143744 | tf_op jit(solution)/shard_map/thd,khd->htk/dot_general | solution.py:121
  160.1 15.2 %fusion = f32[4,256]{1,0:T(4,128)S(1)} fusion(f32[4,256,8192]{2,1,0:T(8,128)} %get-tuple-element.27, f32[4,256]{1,0:T(4,128)S(1)} %max.15, pred[256,8192]{1,0:T(8,128)(4,1)S(1)} %copy-done.4), kind=kLoop, calls=%fused_computation.2 | loop fusion | flops 33553408 | bytes 35659776 | tf_op jit(solution)/shard_map/reduce_sum | solution.py:128
  175.4 15.2 %fusion.28 = bf16[4,256,96]{1,2,0:T(8,128)(2,1)S(1)} fusion(bf16[8192,4,96]{0,2,1:T(8,128)(2,1)} %reshape.236, f32[4,256,8192]{2,1,0:T(8,128)} %get-tuple-element.27, f32[4,256]{1,0:T(4,128)S(1)} %max.15, pred[256,8192]{1,0:T(8,128)(4,1)S(1)} %copy-done.4, f32[4,256,96]{1,2,0:T(8,128)S(1)} %copy.77, f32[4,256]{1,0:T(4,128)S(1)} %get-tuple-element.8, ...), kind=kOutput, calls=%fused_computation.40 | convolution fusion | flops 1644560384 | bytes 42545152 | tf_op jit(solution)/shard_map/htk,khd->htd/dot_general | solution.py:129
  190.7 2.2 convolution_convert_fusion
  192.9 0.0 all-gather.10.cloned.1.call-start
  193.0 0.5 all-gather.10.cloned.1.call-update
  193.6 0.1 convolution_convert_fusion.1
  193.7 18.2 %psum.21 = bf16[256,16]{0,1:T(8,128)(2,1)S(1)} all-reduce(bf16[256,16]{0,1:T(8,128)(2,1)S(1)} %convolution_convert_fusion.1), channel_id=1, replica_groups=mesh['seq'=32,'tensor'=8] {'tensor'}, use_global_device_ids=true, to_apply=%region_10.11 | all-reduce | flops 4096 | bytes 16384 | tf_op jit(solution)/shard_map/psum | solution.py:145
  211.9 114.7 %all-gather.12.cloned.1.call-done = bf16[2048,3072]{1,0:T(8,128)(2,1)} async-done(((bf16[256,3072]{1,0:T(8,128)(2,1)}), bf16[2048,3072]{1,0:T(8,128)(2,1)}) %all-gather.12.cloned.1.call-update) | async-done | bytes 12582928 | tf_op jit(solution)/shard_map/all_gather | solution.py:142
  326.6 8.8 %reduce_sum.118 = bf16[256,3072]{1,0:T(8,128)(2,1)} reduce(bf16[8,256,3072]{2,1,0:T(8,128)(2,1)} %bitcast.56, bf16[]{:T(256)} %constant.87.clone.1), dimensions={0}, to_apply=%region_9.10 | reduce | flops 5505024 | bytes 14155778 | tf_op jit(solution)/shard_map/reduce_sum | solution.py:142
  335.4 2.9 multiply_reduce_fusion.1
  338.3 0.6 multiply_reduce_fusion
  338.9 3.0 multiply_convert_fusion.1
  341.9 53.4 %all-gather.10.cloned.1.call-done = bf16[2048,3072]{0,1:T(8,128)(2,1)} async-done(((bf16[2048,96]{0,1:T(8,128)(2,1)}), bf16[2048,3072]{0,1:T(8,128)(2,1)}) %all-gather.10.cloned.1.call-update) | async-done | bytes 12582928 | tf_op jit(solution)/shard_map/all_gather | solution.py:153
  395.3 11.9 %fusion.60 = (f32[512]{0:T(512)S(1)}, f32[512,2048]{1,0:T(8,128)}) fusion(bf16[2048,3072]{0,1:T(8,128)(2,1)} %all-gather.10.cloned.1.call-done, bf16[256,3072]{1,0:T(8,128)(2,1)} %get-tuple-element.19, bf16[256,3072]{1,0:T(8,128)(2,1)} %get-tuple-element.18), kind=kOutput, calls=%fused_computation.99 | convolution fusion | flops 6449790464 | bytes 19924992 | tf_op jit(solution)/shard_map/dot_general | solution.py:155
  407.2 17.4 %pmax.7 = f32[512]{0:T(512)S(1)} all-reduce(f32[512]{0:T(512)S(1)} %get-tuple-element.30), channel_id=1, replica_groups=mesh['seq'=32,'tensor'=8] {'tensor'}, use_global_device_ids=true, to_apply=%region_16.17 | all-reduce | flops 512 | bytes 4096 | tf_op jit(solution)/shard_map/pmax | solution.py:163
  424.6 3.6 select_reduce_fusion.1
  428.3 15.0 %all-reduce = (f32[512]{0:T(512)S(1)}, f32[512]{0:T(512)S(1)}) all-reduce(f32[512]{0:T(512)S(1)} %get-tuple-element.3, f32[512]{0:T(512)S(1)} %get-tuple-element.2), channel_id=1, replica_groups=mesh['seq'=32,'tensor'=8] {'tensor'}, use_global_device_ids=true, to_apply=%region_18.19 | all-reduce | flops 1024 | bytes 8192 | tf_op jit(solution)/shard_map/psum | solution.py:165
  443.3 0.6 fusion.59
  (45 shorter events, 0.3 us)
Async XLA Ops:
  7.2 183.5 %copy-start = (bf16[384,3072]{1,0:T(8,128)(2,1)S(1)}, bf16[384,3072]{1,0:T(8,128)(2,1)}, u32[]{:S(2)}) copy-start(bf16[384,3072]{1,0:T(8,128)(2,1)} %param.17) | copy-start | bytes 7077892
  7.2 59.8 %all-gather.6.cloned.1.call-start = ((), (), s32[]{:S(2)}) async-start(), calls=%async_computation | async-start | bytes 6488064 | tf_op jit(solution)/shard_map/all_gather | solution.py:103
  7.9 114.8 %all-gather.8.cloned.1.call-start = ((), (), s32[]{:S(2)}) async-start(), calls=%async_computation.1 | async-start | bytes 6488064 | tf_op jit(solution)/shard_map/all_gather | solution.py:104
  8.7 317.9 %all-gather.12.cloned.1.call-start = ((), (), s32[]{:S(2)}) async-start(), calls=%async_computation.3 | async-start | bytes 14155776 | tf_op jit(solution)/shard_map/all_gather | solution.py:142
  19.7 4.3 copy-start.13
  26.2 3.3 copy-start.1
  26.2 3.4 copy-start.5
  30.6 2.8 copy-start.6
  38.4 0.7 copy-start.12
  131.8 10.3 %copy-start.7 = (bf16[256,4,48]{0,2,1:T(8,128)(2,1)S(1)}, bf16[256,4,48]{0,2,1:T(8,128)(2,1)}, u32[]{:S(2)}) copy-start(bf16[256,4,48]{0,2,1:T(8,128)(2,1)} %copy-done.6) | copy-start | bytes 294916
  142.1 18.0 %copy-start.4 = (pred[256,8192]{1,0:T(8,128)(4,1)S(1)}, pred[256,8192]{1,0:T(8,128)(4,1)}, u32[]{:S(2)}) copy-start(pred[256,8192]{1,0:T(8,128)(4,1)} %compare_and_fusion) | copy-start | bytes 6291460
  190.6 2.9 copy-start.10
  190.6 2.9 copy-start.11
  190.6 2.9 copy-start.9
  192.9 202.4 %all-gather.10.cloned.1.call-start = ((), (), s32[]{:S(2)}) async-start(), calls=%async_computation.2 | async-start | bytes 12976128 | tf_op jit(solution)/shard_map/all_gather | solution.py:153
  326.6 8.8 %copy-start.8 = (bf16[16,3072]{1,0:T(8,128)(2,1)S(1)}, bf16[16,3072]{1,0:T(8,128)(2,1)}, u32[]{:S(2)}) copy-start(bf16[16,3072]{1,0:T(8,128)(2,1)} %param.19) | copy-start | bytes 294916
  335.4 2.9 copy-start.2
  335.4 2.9 copy-start.3
Sparse Core Ops, SparseCore 0:
  10.6 56.3 all-gather.5
  69.5 53.1 all-gather.7
  193.0 133.4 all-gather.11
  329.0 66.2 all-gather.9
